TPU v7x, 128 devices: a whole 4x4x4 slice. The times are simulated.
128 devices in a mesh: row: 16 (over z_lo, x, core), col: 8 (over z_hi, y).
Axes of the slice: x: 4, y: 4, z: 4 (z_hi: 2, z_lo: 2; z = z_hi * 2 + z_lo), core: 2. Of those that a mesh axis runs over, the one named last changes fastest.
Arguments:
- right_sides: bfloat16 [4, 24, 1536, 3072], P(None, None, 'row', 'col'), may hold values from -6 to 6
- to_eigen: bfloat16 [1536, 1536], replicated, may hold values from -0.15625 to 0.15625
- from_eigen: bfloat16 [1536, 1536], replicated, may hold values from -0.15625 to 0.15625
- eigenvalues: float32 [1536], replicated, may hold values from 0.05 to 20
Outputs:
- solutions: bfloat16 [4, 24, 1536, 3072], P(None, None, 'row', 'col')
All inputs are finite; a program needn't handle non-finite values.
Results may differ from a plain program's by a relative error of at most 0.0049.
Values may be sent and summed in bfloat16 or wider, within the bound.
A program may use at most 192 MiB of HBM per device.

v0:
```python
import jax
import jax.numpy as jnp
from jax import lax
from jax.sharding import PartitionSpec as P

KX = 24
KZ = 3072


def solve_items(lines, kx_float, kz_float, to_eigen, from_eigen, eigenvalues):
    damping = 4.0 * (kx_float[:, None] ** 2 / (KX * KX) + kz_float[None, :] ** 2 / (KZ * KZ))
    damping_gain = 1.0 / (1.0 + eigenvalues[None, :, None] + damping[:, None, :])
    coefficients = jnp.einsum("mn,gnj->gmj", to_eigen, lines, preferred_element_type=jnp.float32)
    scaled = (coefficients * damping_gain).astype(jnp.bfloat16)
    return jnp.einsum("mn,gnj->gmj", from_eigen, scaled, preferred_element_type=jnp.float32).astype(
        jnp.bfloat16
    )


def on_device(right_sides, to_eigen, from_eigen, eigenvalues):
    lines = lax.all_to_all(
        lax.all_to_all(right_sides, "col", split_axis=1, concat_axis=3, tiled=True),
        "row",
        split_axis=3,
        concat_axis=2,
        tiled=True,
    )
    kx_local = lines.shape[1]
    kz_local = lines.shape[3]
    ny_full = lines.shape[2]
    kx_float = (lax.axis_index("col") * kx_local + jnp.arange(kx_local, dtype=jnp.int32)).astype(
        jnp.float32
    )
    within = jnp.arange(kz_local, dtype=jnp.int32)
    kz_index = lax.axis_index("row") * kz_local + within
    kz_float = kz_index.astype(jnp.float32)
    flat_lines = lines.reshape(4 * kx_local, ny_full, kz_local)
    kx_items = jnp.tile(kx_float, 4)
    solved = solve_items(flat_lines, kx_items, kz_float, to_eigen, from_eigen, eigenvalues).reshape(
        4, kx_local, ny_full, kz_local
    )
    return lax.all_to_all(
        lax.all_to_all(solved, "row", split_axis=2, concat_axis=3, tiled=True),
        "col",
        split_axis=3,
        concat_axis=1,
        tiled=True,
    )


def solution(mesh):
    placed = (P(None, None, "row", "col"), P(), P(), P())
    return jax.shard_map(
        on_device,
        mesh=mesh,
        in_specs=placed,
        out_specs=P(None, None, "row", "col"),
        check_vma=False,
    )
```

profile of v0, /device:TPU:0, one launch (start us, length us, event | category | flops | bytes accessed | tf_op | source)
XLA Modules:
  0.0 580.9 jit_solution(9566069495555122700)
XLA Ops:
  0.0 4.3 copy.21
  4.3 90.3 %all_to_all.69 = bf16[4,24,96,384]{3,2,0,1:T(8,128)(2,1)} all-to-all(bf16[4,24,96,384]{3,2,0,1:T(8,128)(2,1)S(1)} %copy.21), channel_id=1, replica_groups=mesh['row'=16,'col'=8] {'col'}, dimensions={1} | all-to-all | bytes 14155776 | tf_op jit(solution)/shard_map/all_to_all | solution.py:22
  94.6 14.7 %copy.31 = bf16[4,3,96,8,384]{2,0,1,4,3:T(4,128)(2,1)} copy(bf16[4,3,96,8,384]{4,2,0,1,3:T(8,128)(2,1)} %bitcast.48) | data formatting | bytes 14155776 | tf_op jit(solution)/shard_map/all_to_all | solution.py:22
  109.3 0.0 copy-start
  109.3 5.0 all-to-all-start.1
  114.4 0.1 div.19
  114.5 0.0 copy-done
  114.5 0.1 add_multiply_fusion
  114.6 126.7 %all-to-all-done.1 = bf16[4,3,96,3072]{2,0,1,3:T(4,128)(2,1)} async-done(((bf16[4,3,96,3072]{2,0,1,3:T(4,128)(2,1)}), bf16[4,3,96,3072]{2,0,1,3:T(4,128)(2,1)}, u32[]{:S(2)}, u32[]{:S(2)}) %all-to-all-start.1) | async-done | bytes 7077920 | tf_op jit(solution)/shard_map/all_to_all | solution.py:21
  241.3 13.4 %copy.41 = bf16[4,3,96,16,192]{2,3,4,1,0:T(8,128)(2,1)} copy(bf16[4,3,96,16,192]{2,0,1,4,3:T(4,128)(2,1)} %bitcast.3) | data formatting | bytes 14155776 | tf_op jit(solution)/shard_map/all_to_all | solution.py:21
  254.6 16.2 %reshape.59 = bf16[12,1536,192]{1,2,0:T(8,128)(2,1)} reshape(bf16[4,3,16,96,192]{3,2,4,1,0:T(8,128)(2,1)} %bitcast.43) | data formatting | bytes 14155776 | tf_op jit(solution)/shard_map/reshape | solution.py:37
  270.9 29.0 %fusion.3 = bf16[12,192,1536]{2,1,0:T(8,128)(2,1)} fusion(f32[12,192]{1,0:T(8,128)S(1)} %add_multiply_fusion, f32[1536]{0:T(1024)S(1)} %broadcast_add_fusion, bf16[1536,1536]{1,0:T(8,128)(2,1)} %param.6, bf16[12,1536,192]{1,2,0:T(8,128)(2,1)} %reshape.59, bf16[1536,1536]{1,0:T(8,128)(2,1)} %param.5), kind=kOutput, calls=%fused_computation.5 | convolution fusion | flops 21760966656 | bytes 23608320 | tf_op jit(solution)/shard_map/mn,gnj->gmj/dot_general | solution.py:15
  299.9 14.8 %copy.25 = bf16[4,3,1536,192]{3,0,1,2:T(4,128)(2,1)} copy(bf16[4,3,1536,192]{2,3,1,0:T(8,128)(2,1)} %bitcast.49) | data formatting | bytes 14155776 | tf_op jit(solution)/shard_map/reshape | solution.py:39
  314.8 111.0 %all_to_all.70 = bf16[4,3,1536,192]{3,0,1,2:T(4,128)(2,1)} all-to-all(bf16[4,3,1536,192]{3,0,1,2:T(4,128)(2,1)} %copy.25), channel_id=1, replica_groups=mesh['row'=16,'col'=8] {'row'}, dimensions={2} | all-to-all | bytes 14155776 | tf_op jit(solution)/shard_map/all_to_all | solution.py:43
  425.8 12.7 %copy.40 = bf16[4,3,16,96,192]{4,2,3,1,0:T(8,128)(2,1)} copy(bf16[4,3,16,96,192]{4,0,1,3,2:T(4,128)(2,1)} %bitcast.44) | data formatting | bytes 14155776 | tf_op jit(solution)/shard_map/all_to_all | solution.py:43
  438.5 15.2 %copy.34 = bf16[4,3,96,16,192]{2,0,1,4,3:T(4,128)(2,1)} copy(bf16[4,3,96,16,192]{4,3,2,1,0:T(8,128)(2,1)} %bitcast.45) | data formatting | bytes 14155776 | tf_op jit(solution)/shard_map/all_to_all | solution.py:43
  453.7 112.6 %all_to_all.71 = bf16[4,3,96,3072]{2,0,1,3:T(4,128)(2,1)} all-to-all(bf16[4,3,96,3072]{2,0,1,3:T(4,128)(2,1)} %bitcast.46), channel_id=1, replica_groups=mesh['row'=16,'col'=8] {'col'}, dimensions={3} | all-to-all | bytes 14155776 | tf_op jit(solution)/shard_map/all_to_all | solution.py:42
  566.3 14.6 %copy.36 = bf16[4,3,96,8,384]{4,2,1,3,0:T(8,128)(2,1)} copy(bf16[4,3,96,8,384]{2,0,1,4,3:T(4,128)(2,1)} %bitcast.47) | data formatting | bytes 14155776 | tf_op jit(solution)/shard_map/all_to_all | solution.py:42
  (4 shorter events, 0.0 us)
Async XLA Ops:
  109.3 5.2 copy-start
  109.3 131.9 %all-to-all-start.1 = ((bf16[4,3,96,3072]{2,0,1,3:T(4,128)(2,1)}), bf16[4,3,96,3072]{2,0,1,3:T(4,128)(2,1)}, u32[]{:S(2)}, u32[]{:S(2)}) async-start(bf16[4,3,96,3072]{2,0,1,3:T(4,128)(2,1)} %bitcast.42), calls=%async_computation.1 | async-start | bytes 18874368 | tf_op jit(solution)/shard_map/all_to_all | solution.py:21
where the time goes:
time: 583 us; the launch traced here: 581 us
  blocking collectives  314 us (54%)
  waiting for transfers between devices  127 us (22%)
  local copies, waits for them, and re-layouts  106 us (18%)
  matrix products  29 us (5%)
    all_to_all x1, waiting for transfers between devices, on_device(): lax.all_to_all(lax.all_to_all(right_sides, 'col', split_axis=1, concat_ax...  127 us
    all_to_all x1, blocking collectives, on_device(): lax.all_to_all(lax.all_to_all(solved, 'row', split_axis=2, concat_axis=3,...  113 us
    all_to_all x1, blocking collectives, on_device(): lax.all_to_all(solved, 'row', split_axis=2, concat_axis=3, tiled=True)  111 us
    all_to_all x1, blocking collectives, on_device(): lax.all_to_all(right_sides, 'col', split_axis=1, concat_axis=3, tiled=True)  90.3 us
    dot_general x1, matrix products, solve_items(): jnp.einsum('mn,gnj->gmj', from_eigen, scaled, preferred_element_type=jnp....  29 us
    all_to_all x2, local copies, waits for them, and re-layouts, on_device(): lax.all_to_all(solved, 'row', split_axis=2, concat_axis=3, tiled=True)  27.9 us
    reshape x1, local copies, waits for them, and re-layouts, on_device(): flat_lines = lines.reshape(4 * kx_local, ny_full, kz_local)  16.2 us
    reshape x1, local copies, waits for them, and re-layouts, on_device(): solve_items(flat_lines, kx_items, kz_float, to_eigen, from_eigen, eigenva...  14.8 us
  transfers between devices with their start and end apart: 1, of which 1 were waited for; matrix products, arithmetic and copies ran while one was open for 0% of the time, Pallas kernels for 0%

commit v1 on v0

v1 whole, which is shorter than its diff:
```python
import jax
import jax.numpy as jnp
from jax import lax
from jax.sharding import PartitionSpec as P

KX = 24
KZ = 3072


def on_device(right_sides, to_eigen, from_eigen, eigenvalues):
    comps, kx, ny_local, kz_local = right_sides.shape
    planes = comps * kx
    rows = lax.axis_size("row")
    lines = lax.all_to_all(
        right_sides.reshape(planes, ny_local, kz_local),
        "row",
        split_axis=0,
        concat_axis=1,
        tiled=True,
    )
    held = planes // rows
    plane = lax.axis_index("row") * held + jnp.arange(held, dtype=jnp.int32)
    kx_float = (plane % kx).astype(jnp.float32)
    kz_index = lax.axis_index("col") * kz_local + jnp.arange(kz_local, dtype=jnp.int32)
    kz_float = kz_index.astype(jnp.float32)
    damping = 4.0 * (kx_float[:, None] ** 2 / (KX * KX) + kz_float[None, :] ** 2 / (KZ * KZ))
    damping_gain = 1.0 / (1.0 + eigenvalues[None, :, None] + damping[:, None, :])
    coefficients = jnp.einsum("mn,gnj->gmj", to_eigen, lines, preferred_element_type=jnp.float32)
    scaled = (coefficients * damping_gain).astype(jnp.bfloat16)
    solved = jnp.einsum("mn,gnj->gmj", from_eigen, scaled, preferred_element_type=jnp.float32).astype(
        jnp.bfloat16
    )
    back = lax.all_to_all(solved, "row", split_axis=1, concat_axis=0, tiled=True)
    return back.reshape(right_sides.shape)


def solution(mesh):
    placed = (P(None, None, "row", "col"), P(), P(), P())
    return jax.shard_map(
        on_device,
        mesh=mesh,
        in_specs=placed,
        out_specs=P(None, None, "row", "col"),
        check_vma=False,
    )
```

time: 583 us -> 265 us (0.45)
  blocking collectives: 314 us -> 111 us
  local copies, waits for them, and re-layouts: 106 us -> 23.4 us
  waiting for transfers between devices: 127 us -> 95 us
    all_to_all x3 -> x1, blocking collectives: 314 us -> 111 us  [on_device(): lax.all_to_all(solved, 'row', split_axis=1, concat_axis=0, tiled=True)]
    all_to_all x5 -> x2, local copies, waits for them, and re-layouts: 70.6 us -> 11.2 us  [the longest x1 6.92 us: on_device(): lax.all_to_all(right_sides.reshape(planes, ny_local, kz_local), 'row', sp...]
    all_to_all x1, waiting for transfers between devices: 127 us -> 95 us  [on_device(): lax.all_to_all(right_sides.reshape(planes, ny_local, kz_local), 'row', sp...]
    reshape x2 -> x0, local copies, waits for them, and re-layouts: 31.1 us -> none  [the longest x1 16.2 us: on_device(): flat_lines = lines.reshape(4 * kx_local, ny_full, kz_local)]
    convert_element_type x0 -> x1, local copies, waits for them, and re-layouts: none -> 12.2 us  [on_device(): jnp.einsum('mn,gnj->gmj', from_eigen, scaled, preferred_element_type=jnp....]
where the time goes in v1:
time: 265 us; the launch traced here: 264 us
  blocking collectives  111 us (42%)
  waiting for transfers between devices  95 us (36%)
  matrix products  29.1 us (11%)
  local copies, waits for them, and re-layouts  23.4 us (9%)
  starting transfers between devices  6.05 us (2%)
    all_to_all x1, blocking collectives, on_device(): lax.all_to_all(solved, 'row', split_axis=1, concat_axis=0, tiled=True)  111 us
    all_to_all x1, waiting for transfers between devices, on_device(): lax.all_to_all(right_sides.reshape(planes, ny_local, kz_local), 'row', sp...  95 us
    dot_general x1, matrix products, on_device(): jnp.einsum('mn,gnj->gmj', from_eigen, scaled, preferred_element_type=jnp....  29.1 us
    convert_element_type x1, local copies, waits for them, and re-layouts, on_device(): jnp.einsum('mn,gnj->gmj', from_eigen, scaled, preferred_element_type=jnp....  12.2 us
    all_to_all x1, local copies, waits for them, and re-layouts, on_device(): lax.all_to_all(right_sides.reshape(planes, ny_local, kz_local), 'row', sp...  6.92 us
    all_to_all x1, starting transfers between devices, on_device(): lax.all_to_all(right_sides.reshape(planes, ny_local, kz_local), 'row', sp...  6.05 us
  transfers between devices with their start and end apart: 1, of which 1 were waited for; matrix products, arithmetic and copies ran while one was open for 0% of the time, Pallas kernels for 0%

profile of v1, /device:TPU:0, one launch (start us, length us, event | category | flops | bytes accessed | tf_op | source)
XLA Modules:
  0.0 264.4 jit_solution(13368562106753232442)
XLA Ops:
  0.0 0.0 copy-start
  0.0 6.0 %all-to-all-start = ((bf16[96,96,384]{2,1,0:T(8,128)(2,1)}), bf16[96,96,384]{2,1,0:T(8,128)(2,1)}, u32[]{:S(2)}, u32[]{:S(2)}) async-start(bf16[96,96,384]{2,1,0:T(8,128)(2,1)} %bitcast.27), calls=%async_computation | async-start | bytes 14155776 | tf_op jit(solution)/shard_map/all_to_all | solution.py:14
  6.1 0.1 add_multiply_fusion
  6.2 0.0 copy-done
  6.2 95.0 %all-to-all-done = bf16[96,96,384]{2,1,0:T(8,128)(2,1)} async-done(((bf16[96,96,384]{2,1,0:T(8,128)(2,1)}), bf16[96,96,384]{2,1,0:T(8,128)(2,1)}, u32[]{:S(2)}, u32[]{:S(2)}) %all-to-all-start) | async-done | bytes 7077920 | tf_op jit(solution)/shard_map/all_to_all | solution.py:14
  101.1 6.9 %copy.11 = bf16[6,16,96,384]{3,2,1,0:T(8,128)(2,1)} copy(bf16[6,16,96,384]{3,2,0,1:T(8,128)(2,1)} %bitcast.2) | data formatting | bytes 14155776 | tf_op jit(solution)/shard_map/all_to_all | solution.py:14
  108.1 29.1 %convert_bitcast_fusion = bf16[6,1536,384]{1,2,0:T(8,128)(2,1)} fusion(f32[6,384]{1,0:T(8,128)S(1)} %add_multiply_fusion, f32[1536]{0:T(1024)S(1)} %broadcast_add_fusion, bf16[1536,1536]{1,0:T(8,128)(2,1)} %param.6, bf16[6,1536,384]{2,1,0:T(8,128)(2,1)} %bitcast.28, bf16[1536,1536]{1,0:T(8,128)(2,1)} %param.5), kind=kOutput, calls=%fused_computation.2 | convolution fusion | flops 21760966656 | bytes 23608320 | tf_op jit(solution)/shard_map/mn,gnj->gmj/dot_general | solution.py:30
  137.2 12.2 %copy.13 = bf16[6,1536,384]{2,0,1:T(8,128)(2,1)} copy(bf16[6,1536,384]{1,2,0:T(8,128)(2,1)} %convert_bitcast_fusion) | data formatting | bytes 14155776 | tf_op jit(solution)/shard_map/convert_element_type | solution.py:30
  149.4 110.7 %all_to_all.33 = bf16[6,1536,384]{2,0,1:T(8,128)(2,1)S(1)} all-to-all(bf16[6,1536,384]{2,0,1:T(8,128)(2,1)} %copy.13), channel_id=1, replica_groups=mesh['row'=16,'col'=8] {'row'}, dimensions={1} | all-to-all | bytes 14155776 | tf_op jit(solution)/shard_map/all_to_all | solution.py:33
  260.1 4.3 %copy.15 = bf16[16,6,96,384]{3,2,1,0:T(8,128)(2,1)} copy(bf16[16,6,96,384]{3,1,2,0:T(8,128)(2,1)S(1)} %bitcast.26) | data formatting | bytes 14155776 | tf_op jit(solution)/shard_map/all_to_all | solution.py:33
  (3 shorter events, 0.0 us)
Async XLA Ops:
  0.0 6.2 %copy-start = (f32[1536]{0:T(1024)S(1)}, f32[1536]{0:T(1024)}, u32[]{:S(2)}) copy-start(f32[1536]{0:T(1024)} %param.7) | copy-start | bytes 18436
  0.0 101.1 %all-to-all-start = ((bf16[96,96,384]{2,1,0:T(8,128)(2,1)}), bf16[96,96,384]{2,1,0:T(8,128)(2,1)}, u32[]{:S(2)}, u32[]{:S(2)}) async-start(bf16[96,96,384]{2,1,0:T(8,128)(2,1)} %bitcast.27), calls=%async_computation | async-start | bytes 14155776 | tf_op jit(solution)/shard_map/all_to_all | solution.py:14

commit v2 on v1

v2 whole, which is shorter than its diff:
```python
import functools

import jax
import jax.numpy as jnp
from jax import lax
from jax.experimental import pallas as pl
from jax.experimental.pallas import tpu as pltpu
from jax.sharding import PartitionSpec as P

KX = 24
KZ = 3072
MESH = pl.DeviceIdType.MESH
PAIR = 2
TILE = 256


def exchange_kernel(
    rows,
    x_ref,
    to_hbm,
    from_hbm,
    eig_ref,
    out_ref,
    lines,
    solved,
    scaled,
    to_vmem,
    from_vmem,
    weight_sem,
    own_in_sem,
    own_out_sem,
    send_in,
    recv_in,
    send_out,
    recv_out,
):
    planes, ny_local, width = x_ref.shape
    held = planes // rows
    chunks = held // PAIR
    ny = rows * ny_local
    me = lax.axis_index("row")
    col = lax.axis_index("col")
    high, middle, low = me // 8, (me // 2) % 4, me % 2

    def peer(step, sign=1):
        return (
            ((high + step // 4) % 2) * 8
            + ((middle + 4 + sign * (step % 4)) % 4) * 2
            + (low + step // 8) % 2
        )

    def rows_of(device):
        return pl.ds(pl.multiple_of(device * ny_local, ny_local), ny_local)

    def inward(k, step, j, target):
        return pltpu.make_async_remote_copy(
            src_ref=x_ref.at[target * held + k * PAIR + j],
            dst_ref=lines.at[k, rows_of(me), pl.ds(j * width, width)],
            send_sem=send_in.at[k, step, j],
            recv_sem=recv_in.at[k, step, j],
            device_id={"row": target},
            device_id_type=MESH,
        )

    def outward(k, step, j, target):
        return pltpu.make_async_remote_copy(
            src_ref=solved.at[k, rows_of(target), pl.ds(j * width, width)],
            dst_ref=out_ref.at[me * held + k * PAIR + j],
            send_sem=send_out.at[k, step, j],
            recv_sem=recv_out.at[k, step, j],
            device_id={"row": target},
            device_id_type=MESH,
        )

    def own_in(k, j):
        return pltpu.make_async_copy(
            x_ref.at[me * held + k * PAIR + j],
            lines.at[k, rows_of(me), pl.ds(j * width, width)],
            own_in_sem.at[k, j],
        )

    def own_out(k, j):
        return pltpu.make_async_copy(
            solved.at[k, rows_of(me), pl.ds(j * width, width)],
            out_ref.at[me * held + k * PAIR + j],
            own_out_sem.at[k, j],
        )

    load_to = pltpu.make_async_copy(to_hbm, to_vmem, weight_sem.at[0])
    load_from = pltpu.make_async_copy(from_hbm, from_vmem, weight_sem.at[1])

    barrier = pltpu.get_barrier_semaphore()

    @pl.loop(1, rows)
    def _(step):
        pl.semaphore_signal(barrier, inc=1, device_id={"row": peer(step)}, device_id_type=MESH)

    load_to.start()
    load_from.start()
    pl.semaphore_wait(barrier, rows - 1)

    @pl.loop(0, chunks)
    def _(k):
        @pl.loop(1, rows)
        def _(step):
            for j in range(PAIR):
                inward(k, step, j, peer(step)).start()

        for j in range(PAIR):
            own_in(k, j).start()

    load_to.wait()
    load_from.wait()

    kz = (col * width + lax.broadcasted_iota(jnp.int32, (1, width), 1)).astype(jnp.float32)

    @pl.loop(0, chunks)
    def _(k):
        for j in range(PAIR):
            own_in(k, j).wait()

        @pl.loop(1, rows)
        def _(step):
            for j in range(PAIR):
                inward(k, step, j, peer(step)).wait_recv()

        @pl.loop(0, ny // TILE)
        def _(m):
            part = pl.ds(pl.multiple_of(m * TILE, TILE), TILE)
            coefficients = jnp.dot(to_vmem[part, :], lines[k], preferred_element_type=jnp.float32)
            for j in range(PAIR):
                kx = ((me * held + k * PAIR + j) % KX).astype(jnp.float32)
                damping = 4.0 * (kx * kx / (KX * KX) + kz * kz / (KZ * KZ))
                gain = 1.0 / (1.0 + eig_ref[part, :] + damping)
                cols = slice(j * width, (j + 1) * width)
                scaled[part, cols] = (coefficients[:, cols] * gain).astype(jnp.bfloat16)

        @pl.loop(0, ny // TILE)
        def _(m):
            part = pl.ds(pl.multiple_of(m * TILE, TILE), TILE)
            solved[k, part, :] = jnp.dot(
                from_vmem[part, :], scaled[...], preferred_element_type=jnp.float32
            ).astype(jnp.bfloat16)

        @pl.loop(1, rows)
        def _(step):
            for j in range(PAIR):
                outward(k, step, j, peer(step)).start()

        for j in range(PAIR):
            own_out(k, j).start()

    @pl.loop(0, chunks)
    def _(k):
        for j in range(PAIR):
            own_out(k, j).wait()

        @pl.loop(1, rows)
        def _(step):
            for j in range(PAIR):
                inward(k, step, j, peer(step)).wait_send()
                outward(k, step, j, peer(step)).wait()


def on_device(right_sides, to_eigen, from_eigen, eigenvalues):
    comps, kx, ny_local, width = right_sides.shape
    planes = comps * kx
    rows = lax.axis_size("row")
    ny = rows * ny_local
    held = planes // rows
    chunks = held // PAIR
    anywhere = pl.BlockSpec(memory_space=pl.ANY)
    solved = pl.pallas_call(
        functools.partial(exchange_kernel, rows),
        out_shape=jax.ShapeDtypeStruct((planes, ny_local, width), jnp.bfloat16),
        in_specs=[anywhere, anywhere, anywhere, pl.BlockSpec(memory_space=pltpu.VMEM)],
        out_specs=anywhere,
        scratch_shapes=[
            pltpu.VMEM((chunks, ny, PAIR * width), jnp.bfloat16),
            pltpu.VMEM((chunks, ny, PAIR * width), jnp.bfloat16),
            pltpu.VMEM((ny, PAIR * width), jnp.bfloat16),
            pltpu.VMEM((ny, ny), jnp.bfloat16),
            pltpu.VMEM((ny, ny), jnp.bfloat16),
            pltpu.SemaphoreType.DMA((2,)),
            pltpu.SemaphoreType.DMA((chunks, PAIR)),
            pltpu.SemaphoreType.DMA((chunks, PAIR)),
            pltpu.SemaphoreType.DMA((chunks, rows, PAIR)),
            pltpu.SemaphoreType.DMA((chunks, rows, PAIR)),
            pltpu.SemaphoreType.DMA((chunks, rows, PAIR)),
            pltpu.SemaphoreType.DMA((chunks, rows, PAIR)),
        ],
        compiler_params=pltpu.CompilerParams(
            collective_id=0, has_side_effects=True, vmem_limit_bytes=48 * 2**20
        ),
    )(
        right_sides.reshape(planes, ny_local, width),
        to_eigen,
        from_eigen,
        eigenvalues.reshape(ny, 1),
    )
    return solved.reshape(right_sides.shape)


def solution(mesh):
    placed = (P(None, None, "row", "col"), P(), P(), P())
    return jax.shard_map(
        on_device,
        mesh=mesh,
        in_specs=placed,
        out_specs=P(None, None, "row", "col"),
        check_vma=False,
    )
```

time: 265 us -> 183 us (0.69)
  Pallas kernels: 0 us -> 171 us
  blocking collectives: 111 us -> 0 us
  waiting for transfers between devices: 95 us -> 0 us
  matrix products: 29.1 us -> 0 us
  local copies, waits for them, and re-layouts: 23.4 us -> 10.1 us
  starting transfers between devices: 6.05 us -> 0 us
    pallas_call x0 -> x1, Pallas kernels: none -> 171 us  [on_device(): pl.pallas_call(functools.partial(exchange_kernel, rows), out_shape=jax.Sh...]
    all_to_all x1 -> x0, blocking collectives: 111 us -> none  [on_device(): lax.all_to_all(solved, 'row', split_axis=1, concat_axis=0, tiled=True)]
    all_to_all x1 -> x0, waiting for transfers between devices: 95 us -> none  [on_device(): lax.all_to_all(right_sides.reshape(planes, ny_local, kz_local), 'row', sp...]
    dot_general x1 -> x0, matrix products: 29.1 us -> none  [on_device(): jnp.einsum('mn,gnj->gmj', from_eigen, scaled, preferred_element_type=jnp....]
    convert_element_type x1 -> x0, local copies, waits for them, and re-layouts: 12.2 us -> none  [on_device(): jnp.einsum('mn,gnj->gmj', from_eigen, scaled, preferred_element_type=jnp....]
    all_to_all x2 -> x0, local copies, waits for them, and re-layouts: 11.2 us -> none  [the longest x1 6.92 us: on_device(): lax.all_to_all(right_sides.reshape(planes, ny_local, kz_local), 'row', sp...]
    unnamed x2 -> x3, local copies, waits for them, and re-layouts: 0.01 us -> 9.15 us
    all_to_all x1 -> x0, starting transfers between devices: 6.05 us -> none  [on_device(): lax.all_to_all(right_sides.reshape(planes, ny_local, kz_local), 'row', sp...]
  transfers between devices with their start and end apart: 1 -> 0, of which waited for: 1 -> 0; matrix products, arithmetic and copies ran while one was open for 0% -> 0% of each run, Pallas kernels for 0% -> 0%
where the time goes in v2:
time: 183 us; the launch traced here: 181 us
  Pallas kernels  171 us (93%)
  local copies, waits for them, and re-layouts  10.1 us (6%)
    pallas_call x1, Pallas kernels, on_device(): pl.pallas_call(functools.partial(exchange_kernel, rows), out_shape=jax.Sh...  171 us
    unnamed x3, local copies, waits for them, and re-layouts  9.15 us

profile of v2, /device:TPU:0, one launch (start us, length us, event | category | flops | bytes accessed | tf_op | source)
XLA Modules:
  0.0 181.1 jit_solution(3132378406286952080)
XLA Ops:
  0.0 1.0 reshape.12.eig_ref
  1.0 0.0 copy-start
  1.0 2.3 %copy-done = bf16[1536,1536]{1,0:T(8,128)(2,1)S(1)} copy-done((bf16[1536,1536]{1,0:T(8,128)(2,1)S(1)}, bf16[1536,1536]{1,0:T(8,128)(2,1)}, u32[]{:S(2)}) %copy-start) | copy-done | bytes 4718616
  3.3 171.0 %shard_map.46 = bf16[96,96,384]{2,1,0:T(8,128)(2,1)} custom-call(bf16[96,96,384]{2,1,0:T(8,128)(2,1)} %bitcast.3, bf16[1536,1536]{1,0:T(8,128)(2,1)S(1)} %copy-done, bf16[1536,1536]{1,0:T(8,128)(2,1)} %from_hbm.1, f32[1536,1]{1,0:T(8,128)S(1)} %reshape.12.eig_ref), custom_call_target="tpu_custom_call" | custom-call | tf_op jit(solution)/shard_map/pallas_call | solution.py:173
  174.3 6.8 %copy.7 = bf16[4,24,96,384]{3,2,1,0:T(8,128)(2,1)} copy(bf16[4,24,96,384]{3,2,1,0:T(8,128)(2,1)} %bitcast.2) | data formatting | bytes 14155776
Async XLA Ops:
  1.0 2.3 %copy-start = (bf16[1536,1536]{1,0:T(8,128)(2,1)S(1)}, bf16[1536,1536]{1,0:T(8,128)(2,1)}, u32[]{:S(2)}) copy-start(bf16[1536,1536]{1,0:T(8,128)(2,1)} %to_hbm.1) | copy-start | bytes 14155780
